TPU v7x, 512 devices: a whole 4x8x8 slice. The times are simulated.
512 devices in a mesh: seq: 32 (over x, y), grp: 16 (over z, core).
Axes of the slice: x: 4, y: 8, z: 8, core: 2. Of those that a mesh axis runs over, the one named last changes fastest.
Arguments:
- normed_hidden_input: bfloat16 [65536, 4096], P(('grp', 'seq')), may hold values from -6 to 6
- frozen_query_rows: bfloat16 [65536, 4096], P(('grp', 'seq')), may hold values from -16 to 16
- frozen_key_rows: bfloat16 [65536, 1024], P(('grp', 'seq')), may hold values from -16 to 16
- attention_output_gradient: bfloat16 [65536, 4096], P(('grp', 'seq')), may hold values from -0.15625 to 0.15625
- adapter_down_weight: bfloat16 [256, 64, 4096], P('grp', None, 'seq'), may hold values from -0.09375 to 0.09375
- adapter_up_weight: bfloat16 [256, 64, 1024], P('grp', 'seq'), may hold values from -0.75 to 0.75
- segment_adapter_index: int32 [16, 16], replicated, may hold values from 0 to 255, as said below
- segment_block_count: int32 [16, 16], replicated, may hold values from 1 to 16, 32 in all within a row
- adapter_row_index: int32 [256], replicated, may hold values from 0 to 255, as said below
Outputs:
- down_grad: float32 [256, 64, 4096], P('grp', None, 'seq')
- up_grad: float32 [256, 64, 1024], P('grp', 'seq')
Inputs may be any that keep to these rules, and one draw needn't show every extreme that they name: A permutation: adapter a is held in row adapter_row_index[a] of adapter_down_weight and adapter_up_weight. `segment_adapter_index`: call rows g * 16 to (g + 1) * 16 - 1 of adapter_down_weight the rows of index g of grp. In each sequence at most 2 segments use adapters held in the rows of one index of grp, and in every sequence some index holds exactly 2 of them. Tenants may repeat within and across sequences. `segment_block_count`: each row sums to 32; in each row some segment has exactly 16 blocks.
All inputs are finite; a program needn't handle non-finite values.
Results may differ from a plain program's by a relative error of at most 0.0056.
Values may be sent and summed in bfloat16 or wider, within the bound.
No kernel may reach another device: no remote copies, remote signals or barrier semaphores. Data moves between devices by JAX's collectives and lax.ppermute only.
A program may use at most 64 MiB of HBM per device.

v0:
```python
import math
import jax
import jax.numpy as jnp
from jax import lax
from jax.sharding import PartitionSpec as P

HEAD_DIM = 128
BLOCK = 128
QROWS = 512
adapter_scale = 2.0


def attend_head(query_head, key_head, grad_head, segment_ids, query_rows, reach):
    length, head_width = query_head.shape
    padded_keys = jnp.concatenate([jnp.zeros((reach, head_width), key_head.dtype), key_head], 0)
    padded_ids = jnp.concatenate([jnp.full((reach,), -1, jnp.int32), segment_ids], 0)
    window = query_rows + reach
    factor = 1.0 / math.sqrt(head_width)

    def one_block(totals, number):
        offset = number * query_rows
        query_block = lax.dynamic_slice_in_dim(query_head, offset, query_rows, 0)
        grad_block = lax.dynamic_slice_in_dim(grad_head, offset, query_rows, 0)
        key_block = lax.dynamic_slice_in_dim(padded_keys, offset, window, 0)
        key_ids = lax.dynamic_slice_in_dim(padded_ids, offset, window, 0)
        query_ids = lax.dynamic_slice_in_dim(segment_ids, offset, query_rows, 0)
        scores = jnp.dot(query_block, key_block.T, preferred_element_type=jnp.float32) * factor
        query_pos = offset + jnp.arange(query_rows, dtype=jnp.int32)
        key_pos = offset - reach + jnp.arange(window, dtype=jnp.int32)
        allowed = (key_ids[None, :] == query_ids[:, None]) & (
            key_pos[None, :] <= query_pos[:, None]
        )
        scores = jnp.where(allowed, scores, jnp.float32(-1e30))
        highest = jnp.max(scores, axis=1, keepdims=True)
        expo = jnp.exp(scores - highest)
        probabilities = (expo / jnp.sum(expo, axis=1, keepdims=True)).astype(jnp.bfloat16)
        contribution = jnp.dot(probabilities.T, grad_block, preferred_element_type=jnp.float32)
        current = lax.dynamic_slice_in_dim(totals, offset, window, 0)
        totals = lax.dynamic_update_slice_in_dim(totals, current + contribution, offset, 0)
        return (totals, None)

    initial = jnp.zeros((length + reach, head_width), jnp.float32)
    totals, _ = lax.scan(one_block, initial, jnp.arange(length // query_rows, dtype=jnp.int32))
    return totals[reach:].astype(jnp.bfloat16)


def local(
    normed_hidden_input,
    frozen_query_rows,
    frozen_key_rows,
    attention_output_gradient,
    adapter_down_weight,
    adapter_up_weight,
    segment_adapter_index,
    segment_block_count,
    adapter_row_index,
):
    group_count = lax.axis_size("grp")
    shard_count = lax.axis_size("seq")
    group_index = lax.axis_index("grp")
    tokens_here, model_width = normed_hidden_input.shape
    portion_width = adapter_down_weight.shape[2]
    resident_adapters, rank_overall = (adapter_down_weight.shape[0], adapter_down_weight.shape[1])
    rank_portion, value_projection_width = (adapter_up_weight.shape[1], adapter_up_weight.shape[2])
    segments = segment_adapter_index.shape[1]
    capacity = max(2, (segments + group_count - 1) // group_count)
    seq_length = tokens_here * shard_count
    block_total = seq_length // BLOCK
    block_here = tokens_here // BLOCK
    reach = min(16, seq_length // (2 * BLOCK)) * BLOCK
    head_total = frozen_query_rows.shape[1] // HEAD_DIM
    kv_heads = value_projection_width // HEAD_DIM
    heads_here = head_total // shard_count
    group_size = head_total // kv_heads
    slot_total = group_count * capacity
    adapter_ids = jnp.arange(adapter_row_index.shape[0], dtype=jnp.int32)
    slot_of = jnp.sum(
        jnp.where(segment_adapter_index[:, :, None] == adapter_ids, adapter_row_index, 0), axis=2
    )
    owner_group = slot_of // resident_adapters
    local_slot = slot_of % resident_adapters
    order_ids = jnp.arange(segments, dtype=jnp.int32)
    earlier = order_ids[:, None] > order_ids[None, :]
    same_owner = owner_group[:, :, None] == owner_group[:, None, :]
    rank_in_owner = jnp.sum((same_owner & earlier[None]).astype(jnp.int32), axis=2)
    placement = owner_group * capacity + rank_in_owner
    capacity_ids = jnp.arange(capacity, dtype=jnp.int32)
    local_ids = jnp.arange(resident_adapters, dtype=jnp.int32)
    picks = (
        (owner_group == group_index)[:, :, None, None]
        & (rank_in_owner[:, :, None, None] == capacity_ids[:, None])
        & (local_slot[:, :, None, None] == local_ids)
    )
    chooser = jnp.sum(picks.astype(jnp.float32), axis=1)
    selector_half = chooser.astype(jnp.bfloat16)
    send_down = jnp.einsum(
        "pgl,lut->pgut", selector_half, adapter_down_weight, preferred_element_type=jnp.float32
    ).astype(jnp.bfloat16)
    send_up = jnp.einsum(
        "gyv,vmf->gymf", selector_half, adapter_up_weight, preferred_element_type=jnp.float32
    ).astype(jnp.bfloat16)
    fetched_down, fetched_up = (
        lax.all_to_all(send_down, "grp", split_axis=0, concat_axis=0, tiled=True),
        lax.all_to_all(send_up, "grp", split_axis=0, concat_axis=0, tiled=True),
    )
    own_blocks = segment_block_count[group_index]
    ends = jnp.cumsum(own_blocks)
    block_seg = jnp.sum(
        (jnp.arange(block_total, dtype=jnp.int32)[:, None] >= ends[None, :]).astype(jnp.int32),
        axis=1,
    )
    own_place = placement[group_index]
    block_place = jnp.sum(
        jnp.where(block_seg[:, None] == order_ids[None, :], own_place[None, :], 0), axis=1
    )
    block_pick = block_place[:, None] == jnp.arange(slot_total, dtype=jnp.int32)[None, :]
    pick_half = block_pick.astype(jnp.bfloat16)
    segment_ids = jnp.broadcast_to(block_seg[:, None], (block_total, BLOCK)).reshape(seq_length)
    block_down_weight = jnp.einsum(
        "bn,nrd->brd",
        pick_half,
        fetched_down.reshape(slot_total, rank_overall, portion_width),
        preferred_element_type=jnp.float32,
    ).astype(jnp.bfloat16)
    block_up_rows = jnp.einsum(
        "bn,nre->bre",
        pick_half,
        fetched_up.reshape(slot_total, rank_portion, value_projection_width),
        preferred_element_type=jnp.float32,
    ).astype(jnp.bfloat16)
    features = lax.all_to_all(normed_hidden_input, "seq", split_axis=1, concat_axis=0, tiled=True)
    amount = lax.axis_size("seq") * tokens_here
    token_rows = features.reshape(amount // BLOCK, BLOCK, portion_width)
    reduced_rank_part = (
        lax.psum_scatter(
            jnp.einsum(
                "jyw,jaw->jya", token_rows, block_down_weight, preferred_element_type=jnp.float32
            ).reshape(amount, rank_overall),
            "seq",
            scatter_dimension=0,
            tiled=True,
        )
        .astype(jnp.bfloat16)
        .reshape(block_here, BLOCK, rank_overall)
    )
    near_up = lax.all_to_all(block_up_rows, "seq", split_axis=0, concat_axis=1, tiled=True)
    query_grid = frozen_query_rows.reshape(tokens_here, shard_count, heads_here, HEAD_DIM)
    key_grid = jnp.repeat(
        frozen_key_rows.reshape(tokens_here, kv_heads, HEAD_DIM), group_size, axis=1
    ).reshape(tokens_here, shard_count, heads_here, HEAD_DIM)
    grad_grid = attention_output_gradient.reshape(tokens_here, shard_count, heads_here, HEAD_DIM)
    query_all = lax.all_to_all(query_grid, "seq", split_axis=1, concat_axis=0, tiled=True)
    key_all = lax.all_to_all(key_grid, "seq", split_axis=1, concat_axis=0, tiled=True)
    grad_all = lax.all_to_all(grad_grid, "seq", split_axis=1, concat_axis=0, tiled=True)

    def per_head(triple):
        return attend_head(triple[0], triple[1], triple[2], segment_ids, QROWS, reach)

    stacked = (
        jnp.moveaxis(query_all[:, 0], 1, 0),
        jnp.moveaxis(key_all[:, 0], 1, 0),
        jnp.moveaxis(grad_all[:, 0], 1, 0),
    )
    result = lax.map(per_head, stacked)
    head_grads = jnp.moveaxis(result, 0, 1)[:, None]
    token_grads = lax.all_to_all(head_grads, "seq", split_axis=0, concat_axis=1, tiled=True)
    value_grad = jnp.sum(
        token_grads.reshape(tokens_here, kv_heads, group_size, HEAD_DIM), axis=2, dtype=jnp.float32
    )
    value_row_blocks = value_grad.reshape(block_here, BLOCK, value_projection_width).astype(
        jnp.bfloat16
    )
    up_weight_terms = adapter_scale * jnp.einsum(
        "fvg,fvn->fgn", reduced_rank_part, value_row_blocks, preferred_element_type=jnp.float32
    )
    backward_rank_part = (
        adapter_scale
        * jnp.einsum("vaw,vpw->vap", value_row_blocks, near_up, preferred_element_type=jnp.float32)
    ).astype(jnp.bfloat16)
    all_low = lax.all_gather(
        backward_rank_part.reshape(tokens_here, rank_overall), "seq", axis=0, tiled=True
    )
    back_down = jnp.einsum(
        "jcy,jct->jyt",
        all_low.reshape(block_total, BLOCK, rank_overall),
        features.reshape(block_total, BLOCK, portion_width),
        preferred_element_type=jnp.float32,
    )
    back_up = lax.all_to_all(up_weight_terms, "seq", split_axis=1, concat_axis=0, tiled=True)
    pick_full = block_pick.astype(jnp.float32)
    slot_down = jnp.einsum("bn,brd->nrd", pick_full, back_down, precision=lax.Precision.HIGHEST)
    slot_up = jnp.einsum("bn,bre->nre", pick_full, back_up, precision=lax.Precision.HIGHEST)
    return_down, return_up = (
        lax.all_to_all(
            slot_down.reshape(group_count, capacity, rank_overall, portion_width),
            "grp",
            split_axis=0,
            concat_axis=0,
            tiled=True,
        ),
        lax.all_to_all(
            slot_up.reshape(group_count, capacity, rank_portion, value_projection_width),
            "grp",
            split_axis=0,
            concat_axis=0,
            tiled=True,
        ),
    )
    down_grad = jnp.einsum("nca,ncrd->ard", chooser, return_down, precision=lax.Precision.HIGHEST)
    up_grad = jnp.einsum("nca,ncre->are", chooser, return_up, precision=lax.Precision.HIGHEST)
    return (down_grad, up_grad)


def solution(mesh):
    return jax.shard_map(
        local,
        mesh=mesh,
        in_specs=(
            P(("grp", "seq"), None),
            P(("grp", "seq"), None),
            P(("grp", "seq"), None),
            P(("grp", "seq"), None),
            P("grp", None, "seq"),
            P("grp", "seq", None),
            P(),
            P(),
            P(),
        ),
        out_specs=(P("grp", None, "seq"), P("grp", "seq", None)),
        check_vma=False,
    )
```

profile of v0, /device:TPU:1, one launch (start us, length us, event | category | flops | bytes accessed | tf_op | source)
XLA Modules:
  0.0 591.7 jit_solution(1120349917430718640)
XLA Ops:
  11.0 11.8 %all-to-all-start.4 = ((bf16[16,2,2,1024]{3,2,1,0:T(2,128)(2,1)}), bf16[16,2,2,1024]{3,2,1,0:T(2,128)(2,1)S(1)}, u32[]{:S(2)}, u32[]{:S(2)}) async-start(bf16[16,2,2,1024]{3,2,1,0:T(2,128)(2,1)} %copy.109), calls=%async_computation.4 | async-start | bytes 262144 | tf_op jit(solution)/shard_map/all_to_all | solution.py:104
  25.0 7.0 %all-to-all-done.4 = bf16[16,2,2,1024]{3,2,1,0:T(2,128)(2,1)S(1)} async-done(((bf16[16,2,2,1024]{3,2,1,0:T(2,128)(2,1)}), bf16[16,2,2,1024]{3,2,1,0:T(2,128)(2,1)S(1)}, u32[]{:S(2)}, u32[]{:S(2)}) %all-to-all-start.4) | async-done | bytes 131104 | tf_op jit(solution)/shard_map/all_to_all | solution.py:104
  35.5 16.8 %all-to-all-done.8 = bf16[16,2,64,128]{3,2,1,0:T(8,128)(2,1)S(1)} async-done(((bf16[16,2,64,128]{3,2,1,0:T(8,128)(2,1)}), bf16[16,2,64,128]{3,2,1,0:T(8,128)(2,1)S(1)}, u32[]{:S(2)}, u32[]{:S(2)}) %all-to-all-start.8) | async-done | bytes 524320 | tf_op jit(solution)/shard_map/all_to_all | solution.py:103
  53.5 9.7 %all-to-all-start.1 = ((bf16[128,32,1,128]{3,0,2,1:T(8,128)(2,1)}), bf16[128,32,1,128]{3,0,2,1:T(8,128)(2,1)S(1)}, u32[]{:S(2)}, u32[]{:S(2)}) async-start(bf16[128,32,1,128]{3,0,2,1:T(8,128)(2,1)} %bitcast.10), calls=%async_computation.1 | async-start | bytes 2097152 | tf_op jit(solution)/shard_map/all_to_all | solution.py:153
  66.2 25.2 %all-to-all-done.1 = bf16[128,32,1,128]{3,0,2,1:T(8,128)(2,1)S(1)} async-done(((bf16[128,32,1,128]{3,0,2,1:T(8,128)(2,1)}), bf16[128,32,1,128]{3,0,2,1:T(8,128)(2,1)S(1)}, u32[]{:S(2)}, u32[]{:S(2)}) %all-to-all-start.1) | async-done | bytes 1048608 | tf_op jit(solution)/shard_map/all_to_all | solution.py:153
  91.4 5.6 all-to-all-start.2
  99.9 22.2 %all-to-all-done.2 = bf16[128,32,1,128]{3,0,2,1:T(8,128)(2,1)} async-done(((bf16[128,32,1,128]{3,0,2,1:T(8,128)(2,1)}), bf16[128,32,1,128]{3,0,2,1:T(8,128)(2,1)}, u32[]{:S(2)}, u32[]{:S(2)}) %all-to-all-start.2) | async-done | bytes 1048608 | tf_op jit(solution)/shard_map/all_to_all | solution.py:154
  122.2 8.1 %all-to-all-start = ((bf16[128,32,1,128]{3,0,2,1:T(8,128)(2,1)}), bf16[128,32,1,128]{3,0,2,1:T(8,128)(2,1)}, u32[]{:S(2)}, u32[]{:S(2)}) async-start(bf16[128,32,1,128]{3,0,2,1:T(8,128)(2,1)} %copy.101), calls=%async_computation | async-start | bytes 2097152 | tf_op jit(solution)/shard_map/all_to_all | solution.py:152
  135.8 19.1 %all-to-all-done = bf16[128,32,1,128]{3,0,2,1:T(8,128)(2,1)} async-done(((bf16[128,32,1,128]{3,0,2,1:T(8,128)(2,1)}), bf16[128,32,1,128]{3,0,2,1:T(8,128)(2,1)}, u32[]{:S(2)}, u32[]{:S(2)}) %all-to-all-start) | async-done | bytes 1048608 | tf_op jit(solution)/shard_map/all_to_all | solution.py:152
  154.9 8.6 %all-to-all-start.6 = ((bf16[128,32,128]{2,0,1:T(8,128)(2,1)}), bf16[128,32,128]{2,0,1:T(8,128)(2,1)S(1)}, u32[]{:S(2)}, u32[]{:S(2)}) async-start(bf16[128,32,128]{2,0,1:T(8,128)(2,1)} %copy.113), calls=%async_computation.6 | async-start | bytes 2097152 | tf_op jit(solution)/shard_map/all_to_all | solution.py:131
  165.3 67.9 %while.19 = (s32[]{:T(128)}, f32[6144,128]{1,0:T(8,128)}, s32[8]{0:T(128)S(1)}, s32[6144]{0:T(1024)S(1)}, s32[4096]{0:T(1024)S(1)}, /*index=5*/bf16[4096,128]{1,...) while((s32[]{:T(128)}, f32[6144,128]{1,0:T(8,128)}, ...), condition=%wide.region_9.10_spmd, body=%wide.region_6.9_spmd.sunk | while | flops 685836288 | bytes 19343620 | solution.py:43
  187.0 3.8 fusion.64
  195.5 3.8 fusion.64
  204.0 3.8 fusion.64
  238.1 9.2 %all-to-all-start.3 = ((bf16[32,2,8192]{2,1,0:T(2,128)(2,1)}), bf16[32,2,8192]{2,1,0:T(2,128)(2,1)S(1)}, u32[]{:S(2)}, u32[]{:S(2)}) async-start(bf16[32,2,8192]{2,1,0:T(2,128)(2,1)} %reshape.260), calls=%async_computation.3 | async-start | bytes 2097152 | tf_op jit(solution)/shard_map/all_to_all | solution.py:166
  251.6 20.3 %all-to-all-done.3 = bf16[32,2,8192]{2,1,0:T(2,128)(2,1)S(1)} async-done(((bf16[32,2,8192]{2,1,0:T(2,128)(2,1)}), bf16[32,2,8192]{2,1,0:T(2,128)(2,1)S(1)}, u32[]{:S(2)}, u32[]{:S(2)}) %all-to-all-start.3) | async-done | bytes 1048608 | tf_op jit(solution)/shard_map/all_to_all | solution.py:166
  272.9 8.3 %all-to-all-start.5 = ((bf16[32,2,1024]{2,1,0:T(2,128)(2,1)}), bf16[32,2,1024]{2,1,0:T(2,128)(2,1)S(1)}, u32[]{:S(2)}, u32[]{:S(2)}) async-start(bf16[32,2,1024]{2,1,0:T(2,128)(2,1)} %copy.111), calls=%async_computation.5 | async-start | bytes 262144 | tf_op jit(solution)/shard_map/all_to_all | solution.py:146
  281.3 4.3 reshape.261
  288.3 176.5 %reduce-scatter.2.cloned.1.call-done = f32[128,64]{0,1:T(8,128)} async-done(((f32[4096,64]{0,1:T(8,128)}), f32[128,64]{0,1:T(8,128)}) %reduce-scatter.2.cloned.1.call-update) | async-done | bytes 32784 | tf_op jit(solution)/shard_map/reduce_scatter | solution.py:135
  466.8 6.5 %all-to-all-start.9 = ((f32[1,64,1024]{2,0,1:T(1,128)}), f32[1,64,1024]{2,0,1:T(1,128)S(1)}, u32[]{:S(2)}, u32[]{:S(2)}) async-start(f32[1,64,1024]{2,0,1:T(1,128)} %copy.126), calls=%async_computation.10 | async-start | bytes 524288 | tf_op jit(solution)/shard_map/all_to_all | solution.py:189
  473.5 39.6 %all_gather.3 = bf16[4096,64]{0,1:T(8,128)(2,1)S(1)} all-gather(bf16[128,64]{0,1:T(8,128)(2,1)S(1)} %fusion.8), channel_id=1, replica_groups=mesh['seq'=32,'grp'=16] {'seq'}, dimensions={0}, use_global_device_ids=true | all-gather | bytes 540672 | tf_op jit(solution)/shard_map/all_gather | solution.py:180
  515.2 25.0 %all-to-all-start.10 = ((f32[16,2,2,1024]{3,1,2,0:T(2,128)}), f32[16,2,2,1024]{3,1,2,0:T(2,128)S(1)}, u32[]{:S(2)}, u32[]{:S(2)}) async-start(f32[16,2,2,1024]{3,1,2,0:T(2,128)} %copy.128), calls=%async_computation.11 | async-start | bytes 524288 | tf_op jit(solution)/shard_map/all_to_all | solution.py:201
  543.5 8.4 %all-to-all-done.10 = f32[16,2,2,1024]{3,1,2,0:T(2,128)S(1)} async-done(((f32[16,2,2,1024]{3,1,2,0:T(2,128)}), f32[16,2,2,1024]{3,1,2,0:T(2,128)S(1)}, u32[]{:S(2)}, u32[]{:S(2)}) %all-to-all-start.10) | async-done | bytes 262176 | tf_op jit(solution)/shard_map/all_to_all | solution.py:201
  556.7 26.0 %all-to-all-done.7 = f32[16,2,64,128]{3,1,2,0:T(2,128)S(1)} async-done(((f32[16,2,64,128]{3,1,2,0:T(2,128)}), f32[16,2,64,128]{3,1,2,0:T(2,128)S(1)}, u32[]{:S(2)}, u32[]{:S(2)}) %all-to-all-start.7) | async-done | bytes 1048608 | tf_op jit(solution)/shard_map/all_to_all | solution.py:194
  (139 shorter events, 102.4 us)
Async XLA Ops:
  7.2 28.3 %copy-start = (bf16[128,1024]{1,0:T(8,128)(2,1)S(1)}, bf16[128,1024]{1,0:T(8,128)(2,1)}, u32[]{:S(2)}) copy-start(bf16[128,1024]{1,0:T(8,128)(2,1)} %param.13) | copy-start | bytes 786436
  11.0 21.0 %all-to-all-start.4 = ((bf16[16,2,2,1024]{3,2,1,0:T(2,128)(2,1)}), bf16[16,2,2,1024]{3,2,1,0:T(2,128)(2,1)S(1)}, u32[]{:S(2)}, u32[]{:S(2)}) async-start(bf16[16,2,2,1024]{3,2,1,0:T(2,128)(2,1)} %copy.109), calls=%async_computation.4 | async-start | bytes 262144 | tf_op jit(solution)/shard_map/all_to_all | solution.py:104
  32.0 20.3 %all-to-all-start.8 = ((bf16[16,2,64,128]{3,2,1,0:T(8,128)(2,1)}), bf16[16,2,64,128]{3,2,1,0:T(8,128)(2,1)S(1)}, u32[]{:S(2)}, u32[]{:S(2)}) async-start(bf16[16,2,64,128]{3,2,1,0:T(8,128)(2,1)} %copy.122), calls=%async_computation.8 | async-start | bytes 1048576 | tf_op jit(solution)/shard_map/all_to_all | solution.py:103
  53.5 37.9 %all-to-all-start.1 = ((bf16[128,32,1,128]{3,0,2,1:T(8,128)(2,1)}), bf16[128,32,1,128]{3,0,2,1:T(8,128)(2,1)S(1)}, u32[]{:S(2)}, u32[]{:S(2)}) async-start(bf16[128,32,1,128]{3,0,2,1:T(8,128)(2,1)} %bitcast.10), calls=%async_computation.1 | async-start | bytes 2097152 | tf_op jit(solution)/shard_map/all_to_all | solution.py:153
  91.4 30.8 %all-to-all-start.2 = ((bf16[128,32,1,128]{3,0,2,1:T(8,128)(2,1)}), bf16[128,32,1,128]{3,0,2,1:T(8,128)(2,1)}, u32[]{:S(2)}, u32[]{:S(2)}) async-start(bf16[128,32,1,128]{3,0,2,1:T(8,128)(2,1)} %copy.104), calls=%async_computation.2 | async-start | bytes 2097152 | tf_op jit(solution)/shard_map/all_to_all | solution.py:154
  122.2 32.7 %all-to-all-start = ((bf16[128,32,1,128]{3,0,2,1:T(8,128)(2,1)}), bf16[128,32,1,128]{3,0,2,1:T(8,128)(2,1)}, u32[]{:S(2)}, u32[]{:S(2)}) async-start(bf16[128,32,1,128]{3,0,2,1:T(8,128)(2,1)} %copy.101), calls=%async_computation | async-start | bytes 2097152 | tf_op jit(solution)/shard_map/all_to_all | solution.py:152
  134.4 30.9 %copy-start.2 = (s32[32]{0:T(128)}, s32[32]{0:T(128)S(1)}, u32[]{:S(2)}) copy-start(s32[32]{0:T(128)S(1)} %select_reduce_fusion.1) | copy-start | bytes 388
  154.9 83.2 %all-to-all-start.6 = ((bf16[128,32,128]{2,0,1:T(8,128)(2,1)}), bf16[128,32,128]{2,0,1:T(8,128)(2,1)S(1)}, u32[]{:S(2)}, u32[]{:S(2)}) async-start(bf16[128,32,128]{2,0,1:T(8,128)(2,1)} %copy.113), calls=%async_computation.6 | async-start | bytes 2097152 | tf_op jit(solution)/shard_map/all_to_all | solution.py:131
  238.1 12.4 %copy-start.3 = (s32[32]{0:T(128)S(1)}, s32[32]{0:T(128)}, u32[]{:S(2)}) copy-start(s32[32]{0:T(128)} %copy-done.2) | copy-start | bytes 388
  238.1 33.8 %all-to-all-start.3 = ((bf16[32,2,8192]{2,1,0:T(2,128)(2,1)}), bf16[32,2,8192]{2,1,0:T(2,128)(2,1)S(1)}, u32[]{:S(2)}, u32[]{:S(2)}) async-start(bf16[32,2,8192]{2,1,0:T(2,128)(2,1)} %reshape.260), calls=%async_computation.3 | async-start | bytes 2097152 | tf_op jit(solution)/shard_map/all_to_all | solution.py:166
  247.4 217.5 %reduce-scatter.2.cloned.1.call-start = ((), (), s32[]{:S(2)}) async-start(), calls=%async_computation.12 | async-start | bytes 1081344 | tf_op jit(solution)/shard_map/reduce_scatter | solution.py:135
  271.9 1.0 copy-start.1
  272.9 193.9 %all-to-all-start.5 = ((bf16[32,2,1024]{2,1,0:T(2,128)(2,1)}), bf16[32,2,1024]{2,1,0:T(2,128)(2,1)S(1)}, u32[]{:S(2)}, u32[]{:S(2)}) async-start(bf16[32,2,1024]{2,1,0:T(2,128)(2,1)} %copy.111), calls=%async_computation.5 | async-start | bytes 262144 | tf_op jit(solution)/shard_map/all_to_all | solution.py:146
  286.7 227.2 %copy-start.4 = (s32[32]{0:T(128)S(1)}, s32[32]{0:T(128)}, u32[]{:S(2)}) copy-start(s32[32]{0:T(128)} %copy-done.2) | copy-start | bytes 388
  466.8 46.3 %all-to-all-start.9 = ((f32[1,64,1024]{2,0,1:T(1,128)}), f32[1,64,1024]{2,0,1:T(1,128)S(1)}, u32[]{:S(2)}, u32[]{:S(2)}) async-start(f32[1,64,1024]{2,0,1:T(1,128)} %copy.126), calls=%async_computation.10 | async-start | bytes 524288 | tf_op jit(solution)/shard_map/all_to_all | solution.py:189
  515.2 36.7 %all-to-all-start.10 = ((f32[16,2,2,1024]{3,1,2,0:T(2,128)}), f32[16,2,2,1024]{3,1,2,0:T(2,128)S(1)}, u32[]{:S(2)}, u32[]{:S(2)}) async-start(f32[16,2,2,1024]{3,1,2,0:T(2,128)} %copy.128), calls=%async_computation.11 | async-start | bytes 524288 | tf_op jit(solution)/shard_map/all_to_all | solution.py:201
  551.9 30.8 %all-to-all-start.7 = ((f32[16,2,64,128]{3,1,2,0:T(2,128)}), f32[16,2,64,128]{3,1,2,0:T(2,128)S(1)}, u32[]{:S(2)}, u32[]{:S(2)}) async-start(f32[16,2,64,128]{3,1,2,0:T(2,128)} %copy.117), calls=%async_computation.7 | async-start | bytes 2097152 | tf_op jit(solution)/shard_map/all_to_all | solution.py:194
Sparse Core Ops, SparseCore 0:
  252.6 212.2 reduce-scatter.1
where the time goes:
time: 594 us; the launch traced here: 592 us
  waiting for transfers between devices  322 us (54%)
  starting transfers between devices  100 us (17%)
  matrix products  60.2 us (10%)
  blocking collectives  39.6 us (7%)
  local copies, waits for them, and re-layouts  38.2 us (6%)
  between operations  14.4 us (2%)
  other arithmetic  12.6 us (2%)
    reduce_scatter x1, waiting for transfers between devices, local(): lax.psum_scatter(jnp.einsum('jyw,jaw->jya', token_rows, block_down_weight...  177 us
    all_gather x1, blocking collectives, local(): lax.all_gather(backward_rank_part.reshape(tokens_here, rank_overall), 'se...  39.6 us
    dot_general x8, matrix products, one_block(): jnp.dot(probabilities.T, grad_block, preferred_element_type=jnp.float32)  30.3 us
    all_to_all x1, waiting for transfers between devices, local(): lax.all_to_all(slot_down.reshape(group_count, capacity, rank_overall, por...  26 us
    all_to_all x1, waiting for transfers between devices, local(): lax.all_to_all(key_grid, 'seq', split_axis=1, concat_axis=0, tiled=True)  25.2 us
    all_to_all x1, starting transfers between devices, local(): lax.all_to_all(slot_up.reshape(group_count, capacity, rank_portion, value...  25 us
    all_to_all x1, waiting for transfers between devices, local(): lax.all_to_all(grad_grid, 'seq', split_axis=1, concat_axis=0, tiled=True)  22.2 us
    all_to_all x1, waiting for transfers between devices, local(): lax.all_to_all(head_grads, 'seq', split_axis=0, concat_axis=1, tiled=True)  20.3 us
  transfers between devices with their start and end apart: 12, of which 9 were waited for; matrix products, arithmetic and copies ran while one was open for 17% of the time, Pallas kernels for 0%

commit v1 on v0

--- a/solution.py
+++ b/solution.py
@@ -149,7 +149,10 @@
         frozen_key_rows.reshape(tokens_here, kv_heads, HEAD_DIM), group_size, axis=1
     ).reshape(tokens_here, shard_count, heads_here, HEAD_DIM)
     grad_grid = attention_output_gradient.reshape(tokens_here, shard_count, heads_here, HEAD_DIM)
-    query_all = lax.all_to_all(query_grid, "seq", split_axis=1, concat_axis=0, tiled=True)
+    query_all = jnp.concatenate(
+        lax.all_to_all(jnp.stack(jnp.split(query_grid, lax.axis_size("seq"), axis=1)), "seq", 0, 0),
+        axis=0,
+    )
     key_all = lax.all_to_all(key_grid, "seq", split_axis=1, concat_axis=0, tiled=True)
     grad_all = lax.all_to_all(grad_grid, "seq", split_axis=1, concat_axis=0, tiled=True)
 

time: 594 us -> 594 us (level)
    all_to_all x1, waiting for transfers between devices: 19.1 us -> 28.1 us  [local(): lax.all_to_all(jnp.stack(jnp.split(query_grid, lax.axis_size('seq'), axis...]
    unnamed x18 -> x51, local copies, waits for them, and re-layouts: 14.3 us -> 14.6 us
where the time goes in v1:
time: 594 us; the launch traced here: 592 us
  waiting for transfers between devices  321 us (54%)
  starting transfers between devices  100 us (17%)
  matrix products  60.1 us (10%)
  blocking collectives  39.6 us (7%)
  local copies, waits for them, and re-layouts  38.7 us (7%)
  between operations  14.5 us (2%)
  other arithmetic  12.6 us (2%)
    reduce_scatter x1, waiting for transfers between devices, local(): lax.psum_scatter(jnp.einsum('jyw,jaw->jya', token_rows, block_down_weight...  176 us
    all_gather x1, blocking collectives, local(): lax.all_gather(backward_rank_part.reshape(tokens_here, rank_overall), 'se...  39.6 us
    dot_general x8, matrix products, one_block(): jnp.dot(probabilities.T, grad_block, preferred_element_type=jnp.float32)  30.3 us
    all_to_all x1, waiting for transfers between devices, local(): lax.all_to_all(jnp.stack(jnp.split(query_grid, lax.axis_size('seq'), axis...  28.1 us
    all_to_all x1, waiting for transfers between devices, local(): lax.all_to_all(slot_down.reshape(group_count, capacity, rank_overall, por...  26 us
    all_to_all x1, starting transfers between devices, local(): lax.all_to_all(slot_up.reshape(group_count, capacity, rank_portion, value...  25 us
    all_to_all x1, waiting for transfers between devices, local(): lax.all_to_all(key_grid, 'seq', split_axis=1, concat_axis=0, tiled=True)  22.3 us
    all_to_all x1, waiting for transfers between devices, local(): lax.all_to_all(head_grads, 'seq', split_axis=0, concat_axis=1, tiled=True)  20.3 us
  transfers between devices with their start and end apart: 12, of which 9 were waited for; matrix products, arithmetic and copies ran while one was open for 17% of the time, Pallas kernels for 0%

profile of v1, /device:TPU:1, one launch (start us, length us, event | category | flops | bytes accessed | tf_op | source)
XLA Modules:
  0.0 591.8 jit_solution(13728101163112725445)
XLA Ops:
  11.0 11.8 %all-to-all-start.4 = ((bf16[16,2,2,1024]{3,2,1,0:T(2,128)(2,1)}), bf16[16,2,2,1024]{3,2,1,0:T(2,128)(2,1)S(1)}, u32[]{:S(2)}, u32[]{:S(2)}) async-start(bf16[16,2,2,1024]{3,2,1,0:T(2,128)(2,1)} %copy.233), calls=%async_computation.4 | async-start | bytes 262144 | tf_op jit(solution)/shard_map/all_to_all | solution.py:104
  27.0 5.0 all-to-all-done.4
  36.8 15.5 %all-to-all-done.8 = bf16[16,2,64,128]{3,2,1,0:T(8,128)(2,1)S(1)} async-done(((bf16[16,2,64,128]{3,2,1,0:T(8,128)(2,1)}), bf16[16,2,64,128]{3,2,1,0:T(8,128)(2,1)S(1)}, u32[]{:S(2)}, u32[]{:S(2)}) %all-to-all-start.8) | async-done | bytes 524320 | tf_op jit(solution)/shard_map/all_to_all | solution.py:103
  52.3 9.7 %all-to-all-start = ((bf16[32,128,1,1,128]{4,1,3,2,0:T(8,128)(2,1)}), bf16[32,128,1,1,128]{4,1,3,2,0:T(8,128)(2,1)S(1)}, u32[]{:S(2)}, u32[]{:S(2)}) async-start(bf16[32,128,1,1,128]{4,1,3,2,0:T(8,128)(2,1)} %copy.225), calls=%async_computation | async-start | bytes 2097152 | tf_op jit(solution)/shard_map/all_to_all | solution.py:153
  62.1 28.1 %all-to-all-done = bf16[32,128,1,1,128]{4,1,3,2,0:T(8,128)(2,1)S(1)} async-done(((bf16[32,128,1,1,128]{4,1,3,2,0:T(8,128)(2,1)}), bf16[32,128,1,1,128]{4,1,3,2,0:T(8,128)(2,1)S(1)}, u32[]{:S(2)}, u32[]{:S(2)}) %all-to-all-start) | async-done | bytes 1048608 | tf_op jit(solution)/shard_map/all_to_all | solution.py:153
  91.6 5.4 all-to-all-start.1
  100.0 22.3 %all-to-all-done.1 = bf16[128,32,1,128]{3,0,2,1:T(8,128)(2,1)S(1)} async-done(((bf16[128,32,1,128]{3,0,2,1:T(8,128)(2,1)}), bf16[128,32,1,128]{3,0,2,1:T(8,128)(2,1)S(1)}, u32[]{:S(2)}, u32[]{:S(2)}) %all-to-all-start.1) | async-done | bytes 1048608 | tf_op jit(solution)/shard_map/all_to_all | solution.py:156
  122.2 8.1 %all-to-all-start.2 = ((bf16[128,32,1,128]{3,0,2,1:T(8,128)(2,1)}), bf16[128,32,1,128]{3,0,2,1:T(8,128)(2,1)}, u32[]{:S(2)}, u32[]{:S(2)}) async-start(bf16[128,32,1,128]{3,0,2,1:T(8,128)(2,1)} %copy.228), calls=%async_computation.2 | async-start | bytes 2097152 | tf_op jit(solution)/shard_map/all_to_all | solution.py:157
  135.8 19.1 %all-to-all-done.2 = bf16[128,32,1,128]{3,0,2,1:T(8,128)(2,1)} async-done(((bf16[128,32,1,128]{3,0,2,1:T(8,128)(2,1)}), bf16[128,32,1,128]{3,0,2,1:T(8,128)(2,1)}, u32[]{:S(2)}, u32[]{:S(2)}) %all-to-all-start.2) | async-done | bytes 1048608 | tf_op jit(solution)/shard_map/all_to_all | solution.py:157
  154.9 8.6 %all-to-all-start.6 = ((bf16[128,32,128]{2,0,1:T(8,128)(2,1)}), bf16[128,32,128]{2,0,1:T(8,128)(2,1)S(1)}, u32[]{:S(2)}, u32[]{:S(2)}) async-start(bf16[128,32,128]{2,0,1:T(8,128)(2,1)} %copy.237), calls=%async_computation.6 | async-start | bytes 2097152 | tf_op jit(solution)/shard_map/all_to_all | solution.py:131
  165.4 67.9 %while.19 = (s32[]{:T(128)}, f32[6144,128]{1,0:T(8,128)}, s32[8]{0:T(128)S(1)}, s32[6144]{0:T(1024)S(1)}, s32[4096]{0:T(1024)S(1)}, /*index=5*/bf16[4096,128]{1,...) while((s32[]{:T(128)}, f32[6144,128]{1,0:T(8,128)}, ...), condition=%wide.region_9.10_spmd, body=%wide.region_6.9_spmd.sunk | while | flops 685836288 | bytes 19343620 | solution.py:43
  187.0 3.8 fusion.64
  195.5 3.8 fusion.64
  204.1 3.8 fusion.64
  238.2 9.2 %all-to-all-start.3 = ((bf16[32,2,8192]{2,1,0:T(2,128)(2,1)}), bf16[32,2,8192]{2,1,0:T(2,128)(2,1)S(1)}, u32[]{:S(2)}, u32[]{:S(2)}) async-start(bf16[32,2,8192]{2,1,0:T(2,128)(2,1)} %reshape.259), calls=%async_computation.3 | async-start | bytes 2097152 | tf_op jit(solution)/shard_map/all_to_all | solution.py:169
  251.6 20.3 %all-to-all-done.3 = bf16[32,2,8192]{2,1,0:T(2,128)(2,1)S(1)} async-done(((bf16[32,2,8192]{2,1,0:T(2,128)(2,1)}), bf16[32,2,8192]{2,1,0:T(2,128)(2,1)S(1)}, u32[]{:S(2)}, u32[]{:S(2)}) %all-to-all-start.3) | async-done | bytes 1048608 | tf_op jit(solution)/shard_map/all_to_all | solution.py:169
  272.9 8.4 %all-to-all-start.5 = ((bf16[32,2,1024]{2,1,0:T(2,128)(2,1)}), bf16[32,2,1024]{2,1,0:T(2,128)(2,1)S(1)}, u32[]{:S(2)}, u32[]{:S(2)}) async-start(bf16[32,2,1024]{2,1,0:T(2,128)(2,1)} %copy.235), calls=%async_computation.5 | async-start | bytes 262144 | tf_op jit(solution)/shard_map/all_to_all | solution.py:146
  281.3 4.3 reshape.260
  288.4 176.3 %reduce-scatter.2.cloned.1.call-done = f32[128,64]{0,1:T(8,128)} async-done(((f32[4096,64]{0,1:T(8,128)}), f32[128,64]{0,1:T(8,128)}) %reduce-scatter.2.cloned.1.call-update) | async-done | bytes 32784 | tf_op jit(solution)/shard_map/reduce_scatter | solution.py:135
  466.6 6.7 %all-to-all-start.9 = ((f32[1,64,1024]{2,0,1:T(1,128)}), f32[1,64,1024]{2,0,1:T(1,128)S(1)}, u32[]{:S(2)}, u32[]{:S(2)}) async-start(f32[1,64,1024]{2,0,1:T(1,128)} %copy.250), calls=%async_computation.10 | async-start | bytes 524288 | tf_op jit(solution)/shard_map/all_to_all | solution.py:192
  473.6 39.6 %all_gather.3 = bf16[4096,64]{0,1:T(8,128)(2,1)S(1)} all-gather(bf16[128,64]{0,1:T(8,128)(2,1)S(1)} %fusion.8), channel_id=1, replica_groups=mesh['seq'=32,'grp'=16] {'seq'}, dimensions={0}, use_global_device_ids=true | all-gather | bytes 540672 | tf_op jit(solution)/shard_map/all_gather | solution.py:183
  515.2 25.0 %all-to-all-start.10 = ((f32[16,2,2,1024]{3,1,2,0:T(2,128)}), f32[16,2,2,1024]{3,1,2,0:T(2,128)S(1)}, u32[]{:S(2)}, u32[]{:S(2)}) async-start(f32[16,2,2,1024]{3,1,2,0:T(2,128)} %copy.252), calls=%async_computation.11 | async-start | bytes 524288 | tf_op jit(solution)/shard_map/all_to_all | solution.py:204
  543.5 8.4 %all-to-all-done.10 = f32[16,2,2,1024]{3,1,2,0:T(2,128)S(1)} async-done(((f32[16,2,2,1024]{3,1,2,0:T(2,128)}), f32[16,2,2,1024]{3,1,2,0:T(2,128)S(1)}, u32[]{:S(2)}, u32[]{:S(2)}) %all-to-all-start.10) | async-done | bytes 262176 | tf_op jit(solution)/shard_map/all_to_all | solution.py:204
  556.8 26.0 %all-to-all-done.7 = f32[16,2,64,128]{3,1,2,0:T(2,128)S(1)} async-done(((f32[16,2,64,128]{3,1,2,0:T(2,128)}), f32[16,2,64,128]{3,1,2,0:T(2,128)S(1)}, u32[]{:S(2)}, u32[]{:S(2)}) %all-to-all-start.7) | async-done | bytes 1048608 | tf_op jit(solution)/shard_map/all_to_all | solution.py:197
  (173 shorter events, 102.9 us)
Async XLA Ops:
  7.2 54.8 %copy-start = (bf16[128,1024]{1,0:T(8,128)(2,1)S(1)}, bf16[128,1024]{1,0:T(8,128)(2,1)}, u32[]{:S(2)}) copy-start(bf16[128,1024]{1,0:T(8,128)(2,1)} %param.13) | copy-start | bytes 786436
  11.0 21.0 %all-to-all-start.4 = ((bf16[16,2,2,1024]{3,2,1,0:T(2,128)(2,1)}), bf16[16,2,2,1024]{3,2,1,0:T(2,128)(2,1)S(1)}, u32[]{:S(2)}, u32[]{:S(2)}) async-start(bf16[16,2,2,1024]{3,2,1,0:T(2,128)(2,1)} %copy.233), calls=%async_computation.4 | async-start | bytes 262144 | tf_op jit(solution)/shard_map/all_to_all | solution.py:104
  32.0 20.3 %all-to-all-start.8 = ((bf16[16,2,64,128]{3,2,1,0:T(8,128)(2,1)}), bf16[16,2,64,128]{3,2,1,0:T(8,128)(2,1)S(1)}, u32[]{:S(2)}, u32[]{:S(2)}) async-start(bf16[16,2,64,128]{3,2,1,0:T(8,128)(2,1)} %copy.246), calls=%async_computation.8 | async-start | bytes 1048576 | tf_op jit(solution)/shard_map/all_to_all | solution.py:103
  52.3 37.9 %all-to-all-start = ((bf16[32,128,1,1,128]{4,1,3,2,0:T(8,128)(2,1)}), bf16[32,128,1,1,128]{4,1,3,2,0:T(8,128)(2,1)S(1)}, u32[]{:S(2)}, u32[]{:S(2)}) async-start(bf16[32,128,1,1,128]{4,1,3,2,0:T(8,128)(2,1)} %copy.225), calls=%async_computation | async-start | bytes 2097152 | tf_op jit(solution)/shard_map/all_to_all | solution.py:153
  90.2 1.4 copy-start.2
  91.6 30.7 %all-to-all-start.1 = ((bf16[128,32,1,128]{3,0,2,1:T(8,128)(2,1)}), bf16[128,32,1,128]{3,0,2,1:T(8,128)(2,1)S(1)}, u32[]{:S(2)}, u32[]{:S(2)}) async-start(bf16[128,32,1,128]{3,0,2,1:T(8,128)(2,1)} %bitcast.71), calls=%async_computation.1 | async-start | bytes 2097152 | tf_op jit(solution)/shard_map/all_to_all | solution.py:156
  122.2 32.7 %all-to-all-start.2 = ((bf16[128,32,1,128]{3,0,2,1:T(8,128)(2,1)}), bf16[128,32,1,128]{3,0,2,1:T(8,128)(2,1)}, u32[]{:S(2)}, u32[]{:S(2)}) async-start(bf16[128,32,1,128]{3,0,2,1:T(8,128)(2,1)} %copy.228), calls=%async_computation.2 | async-start | bytes 2097152 | tf_op jit(solution)/shard_map/all_to_all | solution.py:157
  134.5 30.9 %copy-start.3 = (s32[32]{0:T(128)}, s32[32]{0:T(128)S(1)}, u32[]{:S(2)}) copy-start(s32[32]{0:T(128)S(1)} %select_reduce_fusion.1) | copy-start | bytes 388
  154.9 83.2 %all-to-all-start.6 = ((bf16[128,32,128]{2,0,1:T(8,128)(2,1)}), bf16[128,32,128]{2,0,1:T(8,128)(2,1)S(1)}, u32[]{:S(2)}, u32[]{:S(2)}) async-start(bf16[128,32,128]{2,0,1:T(8,128)(2,1)} %copy.237), calls=%async_computation.6 | async-start | bytes 2097152 | tf_op jit(solution)/shard_map/all_to_all | solution.py:131
  238.2 12.4 %copy-start.4 = (s32[32]{0:T(128)S(1)}, s32[32]{0:T(128)}, u32[]{:S(2)}) copy-start(s32[32]{0:T(128)} %copy-done.3) | copy-start | bytes 388
  238.2 33.7 %all-to-all-start.3 = ((bf16[32,2,8192]{2,1,0:T(2,128)(2,1)}), bf16[32,2,8192]{2,1,0:T(2,128)(2,1)S(1)}, u32[]{:S(2)}, u32[]{:S(2)}) async-start(bf16[32,2,8192]{2,1,0:T(2,128)(2,1)} %reshape.259), calls=%async_computation.3 | async-start | bytes 2097152 | tf_op jit(solution)/shard_map/all_to_all | solution.py:169
  247.4 217.3 %reduce-scatter.2.cloned.1.call-start = ((), (), s32[]{:S(2)}) async-start(), calls=%async_computation.12 | async-start | bytes 1081344 | tf_op jit(solution)/shard_map/reduce_scatter | solution.py:135
  271.9 1.0 copy-start.1
  272.9 193.7 %all-to-all-start.5 = ((bf16[32,2,1024]{2,1,0:T(2,128)(2,1)}), bf16[32,2,1024]{2,1,0:T(2,128)(2,1)S(1)}, u32[]{:S(2)}, u32[]{:S(2)}) async-start(bf16[32,2,1024]{2,1,0:T(2,128)(2,1)} %copy.235), calls=%async_computation.5 | async-start | bytes 262144 | tf_op jit(solution)/shard_map/all_to_all | solution.py:146
  286.8 227.2 %copy-start.5 = (s32[32]{0:T(128)S(1)}, s32[32]{0:T(128)}, u32[]{:S(2)}) copy-start(s32[32]{0:T(128)} %copy-done.3) | copy-start | bytes 388
  466.6 46.6 %all-to-all-start.9 = ((f32[1,64,1024]{2,0,1:T(1,128)}), f32[1,64,1024]{2,0,1:T(1,128)S(1)}, u32[]{:S(2)}, u32[]{:S(2)}) async-start(f32[1,64,1024]{2,0,1:T(1,128)} %copy.250), calls=%async_computation.10 | async-start | bytes 524288 | tf_op jit(solution)/shard_map/all_to_all | solution.py:192
  515.2 36.7 %all-to-all-start.10 = ((f32[16,2,2,1024]{3,1,2,0:T(2,128)}), f32[16,2,2,1024]{3,1,2,0:T(2,128)S(1)}, u32[]{:S(2)}, u32[]{:S(2)}) async-start(f32[16,2,2,1024]{3,1,2,0:T(2,128)} %copy.252), calls=%async_computation.11 | async-start | bytes 524288 | tf_op jit(solution)/shard_map/all_to_all | solution.py:204
  552.0 30.8 %all-to-all-start.7 = ((f32[16,2,64,128]{3,1,2,0:T(2,128)}), f32[16,2,64,128]{3,1,2,0:T(2,128)S(1)}, u32[]{:S(2)}, u32[]{:S(2)}) async-start(f32[16,2,64,128]{3,1,2,0:T(2,128)} %copy.241), calls=%async_computation.7 | async-start | bytes 2097152 | tf_op jit(solution)/shard_map/all_to_all | solution.py:197
Sparse Core Ops, SparseCore 0:
  252.6 212.0 reduce-scatter.1
